TPU v7x, 256 devices: a whole 4x4x8 slice. The times are simulated.
256 devices in a mesh: seq: 64 (over y, z, core), tp: 4 (over x).
Axes of the slice: x: 4, y: 4, z: 8, core: 2. Of those that a mesh axis runs over, the one named last changes fastest.
Arguments:
- short_hidden: bfloat16 [1024, 1280], P('seq', 'tp'), may hold values from -6 to 6
- long_hidden: bfloat16 [4, 1280], P(None, 'tp'), may hold values from -6 to 6
- short_len: int32 [1024], replicated, may hold values from 1 to 127
- short_slot: int32 [1024], replicated, may hold values from 0 to 2047, as said below
- w_query: bfloat16 [1280, 1280], P(None, 'tp'), may hold values from -0.15625 to 0.15625
- w_key: bfloat16 [1280, 1280], P(None, 'tp'), may hold values from -0.15625 to 0.15625
- w_value: bfloat16 [1280, 1280], P(None, 'tp'), may hold values from -0.15625 to 0.15625
- w_out: bfloat16 [1280, 1280], P('tp'), may hold values from -0.15625 to 0.15625
- qk_gain: float32 [1280], P('tp'), may hold values from 0.7 to 2
- step_rate: float32 [1280], replicated, may hold values from 0.1 to 0.6
- short_keys: bfloat16 [2048, 128, 1280], P('seq', None, 'tp'), may hold values from -0.19921875 to 0.19921875
- short_values: bfloat16 [2048, 128, 1280], P('seq', None, 'tp'), may hold values from -6 to 6
- long_keys: bfloat16 [4, 32768, 1280], P(None, 'seq', 'tp'), may hold values from -0.19921875 to 0.19921875
- long_values: bfloat16 [4, 32768, 1280], P(None, 'seq', 'tp'), may hold values from -6 to 6
Outputs:
- short_out: bfloat16 [1024, 1280], P('seq', 'tp')
- long_out: bfloat16 [4, 1280], P(None, 'tp')
Inputs may be any that keep to these rules, and one draw needn't show every extreme that they name: `short_slot`: all slot numbers are distinct; slot s is row s of short_keys and short_values, so it lies on index s // 32 of seq. In every draw some index of seq has all 32 of its slots taken.
All inputs are finite; a program needn't handle non-finite values.
Results may differ from a plain program's by a relative error of at most 0.01.
Values may be sent and summed in bfloat16 or wider, within the bound.
A program may use at most 64 MiB of HBM per device.

v0:
```python
import math
import jax
import jax.numpy as jnp
from jax import lax
from jax.sharding import PartitionSpec as P

HEAD = 64
EPS = 1e-06


def head_unit(x, gain):
    count = x.shape[0]
    parts = x.reshape(count, -1, HEAD)
    parts = parts * lax.rsqrt(jnp.sum(parts * parts, -1, keepdims=True) + EPS)
    return parts.reshape(count, -1) * gain


def row_unit(x):
    return x * lax.rsqrt(jnp.mean(x * x, -1, keepdims=True) + EPS)


def cache_terms(query, keys, values, live):
    batch, positions, width = keys.shape
    key_heads = keys.reshape(batch, positions, width // HEAD, HEAD)
    value_heads = values.reshape(batch, positions, width // HEAD, HEAD)
    query_heads = query.reshape(batch, width // HEAD, HEAD)
    scores = jnp.einsum(
        "bhe,bphe->bhp", query_heads, key_heads, preferred_element_type=jnp.float32
    ) * math.sqrt(HEAD)
    weights = jnp.where(live[:, None, :], jnp.exp(scores), jnp.float32(0.0))
    den = jnp.sum(weights, -1)
    num = jnp.einsum(
        "bhp,bphe->bhe",
        weights.astype(jnp.bfloat16),
        value_heads,
        preferred_element_type=jnp.float32,
    )
    return (num.reshape(batch, width), den)


def on_device(
    short_hidden,
    long_hidden,
    short_len,
    short_slot,
    w_query,
    w_key,
    w_value,
    w_out,
    qk_gain,
    step_rate,
    short_keys,
    short_values,
    long_keys,
    long_values,
):
    full_short, full_long = (
        lax.all_gather(short_hidden, "tp", axis=1, tiled=True),
        lax.all_gather(long_hidden, "tp", axis=1, tiled=True),
    )
    rows = jnp.concatenate([full_short, full_long], 0)
    n_short = full_short.shape[0]
    count = rows.shape[0]
    width = w_query.shape[1]
    head_count = width // HEAD
    q_proj = jnp.dot(rows, w_query, preferred_element_type=jnp.float32)
    k_proj = jnp.dot(rows, w_key, preferred_element_type=jnp.float32)
    v_proj = jnp.dot(rows, w_value, preferred_element_type=jnp.float32)
    query = head_unit(q_proj, qk_gain).astype(jnp.bfloat16)
    new_key = head_unit(k_proj, qk_gain).astype(jnp.bfloat16)
    new_value = v_proj.astype(jnp.bfloat16)
    all_queries = lax.all_gather(query[:n_short], "seq", axis=0, tiled=True)
    total_short = all_queries.shape[0]
    seq_index = lax.axis_index("seq")
    slot_dev = short_keys.shape[0]
    capacity = short_keys.shape[1]
    local_ids = seq_index * slot_dev + jnp.arange(slot_dev, dtype=jnp.int32)
    match = short_slot[None, :] == local_ids[:, None]
    owner = jnp.sum(jnp.where(match, jnp.arange(total_short, dtype=jnp.int32)[None, :], 0), 1)
    filled = jnp.any(match, 1)
    slot_query = jnp.where(
        filled[:, None], jnp.take(all_queries, owner, axis=0), jnp.zeros((), jnp.bfloat16)
    )
    slot_len = jnp.where(filled, jnp.take(short_len, owner, axis=0), 0)
    live = jnp.arange(capacity, dtype=jnp.int32)[None, :] < slot_len[:, None]
    slot_num, slot_den = cache_terms(slot_query, short_keys, short_values, live)
    home_slot = lax.dynamic_slice_in_dim(short_slot, seq_index * n_short, n_short)
    every_num, every_den = (
        lax.all_gather(slot_num.astype(jnp.bfloat16), "seq", axis=0, tiled=True).astype(
            slot_num.dtype
        ),
        lax.all_gather(slot_den.astype(jnp.bfloat16), "seq", axis=0, tiled=True).astype(
            slot_den.dtype
        ),
    )
    short_num = jnp.take(every_num, home_slot, axis=0)
    short_den = jnp.take(every_den, home_slot, axis=0)
    long_count = full_long.shape[0]
    long_live = jnp.ones((long_count, long_keys.shape[1]), dtype=bool)
    long_part_num, long_part_den = cache_terms(query[n_short:], long_keys, long_values, long_live)
    long_num, long_den = lax.psum((long_part_num, long_part_den), "seq")
    cache_num = jnp.concatenate([short_num, long_num], 0).reshape(count, head_count, HEAD)
    cache_den = jnp.concatenate([short_den, long_den], 0)
    query_heads = query.reshape(count, head_count, HEAD)
    key_heads = new_key.reshape(count, head_count, HEAD)
    value_heads = new_value.reshape(count, head_count, HEAD).astype(jnp.float32)
    own = jnp.exp(
        jnp.einsum("rhe,rhe->rh", query_heads, key_heads, preferred_element_type=jnp.float32)
        * math.sqrt(HEAD)
    )
    den = cache_den + own
    num = cache_num + own.astype(jnp.bfloat16).astype(jnp.float32)[..., None] * value_heads
    attended = (num / den[..., None]).reshape(count, width).astype(jnp.bfloat16)
    partial_proj = jnp.dot(attended, w_out, preferred_element_type=jnp.float32)
    tp_index = lax.axis_index("tp")
    proj = lax.psum(partial_proj.astype(jnp.bfloat16), "tp").astype(jnp.float32)
    state = rows.astype(jnp.float32)
    update = state + step_rate * (row_unit(proj) - state)
    result = lax.dynamic_slice_in_dim(row_unit(update), tp_index * width, width, 1)
    result = result.astype(jnp.bfloat16)
    return (result[:n_short], result[n_short:])


def solution(mesh):
    return jax.shard_map(
        on_device,
        mesh=mesh,
        in_specs=(
            P("seq", "tp"),
            P(None, "tp"),
            P(),
            P(),
            P(None, "tp"),
            P(None, "tp"),
            P(None, "tp"),
            P("tp", None),
            P("tp"),
            P(),
            P("seq", None, "tp"),
            P("seq", None, "tp"),
            P(None, "seq", "tp"),
            P(None, "seq", "tp"),
        ),
        out_specs=(P("seq", "tp"), P(None, "tp")),
        check_vma=False,
    )
```

profile of v0, /device:TPU:8, one launch (start us, length us, event | category | flops | bytes accessed | tf_op | source)
XLA Modules:
  0.0 436.6 jit_solution(15223891977575141921)
XLA Ops:
  7.3 1.0 fusion.5
  8.3 0.9 compare_reduce_fusion
  9.2 1.4 gather_fusion
  10.7 12.4 %all-gather.1 = bf16[4,320,4]{1,2,0:T(4,128)(2,1)S(1)} all-gather(bf16[1,320,4]{1,2,0:T(4,128)(2,1)} %bitcast.82), channel_id=1, replica_groups=mesh['seq'=64,'tp'=4] {'tp'}, dimensions={0}, use_global_device_ids=true | all-gather | bytes 12800 | tf_op jit(solution)/shard_map/all_gather | solution.py:59
  23.2 12.1 %all-gather = bf16[4,320,16]{1,2,0:T(8,128)(2,1)S(1)} all-gather(bf16[1,320,16]{1,2,0:T(8,128)(2,1)} %bitcast.80), channel_id=1, replica_groups=mesh['seq'=64,'tp'=4] {'tp'}, dimensions={0}, use_global_device_ids=true | all-gather | bytes 51200 | tf_op jit(solution)/shard_map/all_gather | solution.py:58
  35.4 1.5 fusion.39
  37.3 1.5 fusion.38
  39.1 53.5 %all_gather.17 = bf16[1024,320]{1,0:T(8,128)(2,1)S(1)} all-gather(bf16[16,320]{1,0:T(8,128)(2,1)S(1)} %slice.24), channel_id=1, replica_groups=mesh['seq'=64,'tp'=4] {'seq'}, dimensions={0}, use_global_device_ids=true | all-gather | bytes 665600 | tf_op jit(solution)/shard_map/all_gather | solution.py:72
  92.7 0.6 gather_fusion.1
  93.4 0.1 select_bitcast_fusion
  93.6 0.8 fusion.13
  94.3 0.1 fusion.17
  94.5 0.7 copy-done.3
  95.1 1.5 fusion.11
  96.6 0.7 convert_element_type.59
  97.4 1.6 fusion.40
  99.0 0.1 fusion.27
  99.1 1.8 fusion.19
  101.0 214.0 %all-reduce = (f32[4,5]{0,1:T(8,128)S(1)}, f32[4,320]{1,0:T(4,128)S(1)}) all-reduce(f32[4,5]{0,1:T(8,128)S(1)} %get-tuple-element.13, f32[4,320]{1,0:T(4,128)S(1)} %reshape.148), channel_id=1, replica_groups=mesh['seq'=64,'tp'=4] {'seq'}, use_global_device_ids=true, to_apply=%region_7.8 | all-reduce | flops 1300 | bytes 10400 | tf_op jit(solution)/shard_map/psum | solution.py:101
  315.4 82.4 %all-gather.2 = bf16[64,32,5]{1,2,0:T(8,128)(2,1)S(1)} all-gather(bf16[1,32,5]{1,2,0:T(8,128)(2,1)S(1)} %bitcast.81), channel_id=1, replica_groups=mesh['seq'=64,'tp'=4] {'seq'}, dimensions={0}, use_global_device_ids=true | all-gather | bytes 20800 | tf_op jit(solution)/shard_map/all_gather | solution.py:92
  397.8 0.1 copy.41
  397.9 1.8 copy.60
  399.8 0.8 compare_and_fusion.1
  400.5 1.8 gather_fusion.3
  403.1 3.3 convert_element_type.60
  406.4 2.5 gather_fusion.2
  408.9 2.1 convolution_convert_fusion
  411.1 17.1 %psum.23 = bf16[20,1280]{1,0:T(8,128)(2,1)S(1)} all-reduce(bf16[20,1280]{1,0:T(8,128)(2,1)S(1)} %convolution_convert_fusion), channel_id=1, replica_groups=mesh['seq'=64,'tp'=4] {'tp'}, use_global_device_ids=true, to_apply=%region_8.9 | all-reduce | flops 25600 | bytes 102400 | tf_op jit(solution)/shard_map/psum | solution.py:116
  428.2 0.1 fusion.7
  428.3 0.2 multiply_reduce_fusion
  428.6 0.6 slice.27
  429.2 0.6 slice.26
  (55 shorter events, 2.7 us)
Async XLA Ops:
  7.2 86.4 %copy-start = (bf16[32,128,320]{1,2,0:T(8,128)(2,1)S(1)}, bf16[32,128,320]{1,2,0:T(8,128)(2,1)}, u32[]{:S(2)}) copy-start(bf16[32,128,320]{1,2,0:T(8,128)(2,1)} %param.24) | copy-start | bytes 7864324
  7.2 31.9 %copy-start.2 = (f32[320]{0:T(512)S(1)}, f32[320]{0:T(512)}, u32[]{:S(2)}) copy-start(f32[320]{0:T(512)} %param.22) | copy-start | bytes 3844
  7.2 395.9 %all-gather.5.cloned.1.call-start = ((), (), s32[]{:S(2)}) async-start(), calls=%async_computation | async-start | bytes 1597440 | tf_op jit(solution)/shard_map/all_gather | solution.py:89
  93.4 1.7 copy-start.3
  403.1 25.2 %copy-start.1 = (f32[1280]{0:T(1024)S(1)}, f32[1280]{0:T(1024)}, u32[]{:S(2)}) copy-start(f32[1280]{0:T(1024)} %param.23) | copy-start | bytes 15364
Sparse Core Ops, SparseCore 0:
  97.5 73.4 all-gather.4
where the time goes:
time: 437 us
  blocking collectives  392 us (90%)
  between operations  14.3 us (3%)
  local copies, waits for them, and re-layouts  12.6 us (3%)
  matrix products  10.7 us (2%)
  other arithmetic  7.42 us (2%)
    psum x1, blocking collectives, on_device(): long_num, long_den = lax.psum((long_part_num, long_part_den), 'seq')  214 us
    all_gather x1, blocking collectives, on_device(): lax.all_gather(slot_den.astype(jnp.bfloat16), 'seq', axis=0, tiled=True)  82.4 us
    all_gather x1, blocking collectives, on_device(): all_queries = lax.all_gather(query[:n_short], 'seq', axis=0, tiled=True)  53.5 us
    psum x1, blocking collectives, on_device(): proj = lax.psum(partial_proj.astype(jnp.bfloat16), 'tp').astype(jnp.float32)  17.1 us
    all_gather x1, blocking collectives, on_device(): lax.all_gather(long_hidden, 'tp', axis=1, tiled=True)  12.4 us
    all_gather x1, blocking collectives, on_device(): lax.all_gather(short_hidden, 'tp', axis=1, tiled=True)  12.1 us
  transfers between devices with their start and end apart: 1, of which 0 were waited for; matrix products, arithmetic and copies ran while one was open for 2% of the time, Pallas kernels for 0%

commit v1 on v0

--- a/solution.py
+++ b/solution.py
@@ -6,6 +6,13 @@
 
 HEAD = 64
 EPS = 1e-06
+
+
+def all_by_exchange(x, axis, along):
+    n_dev = lax.axis_size(axis)
+    blocks = jnp.stack([x for _ in range(n_dev)])
+    blocks = lax.all_to_all(blocks, axis, split_axis=0, concat_axis=0)
+    return jnp.concatenate(blocks, axis=along)
 
 
 def head_unit(x, gain):
@@ -89,9 +96,7 @@
         lax.all_gather(slot_num.astype(jnp.bfloat16), "seq", axis=0, tiled=True).astype(
             slot_num.dtype
         ),
-        lax.all_gather(slot_den.astype(jnp.bfloat16), "seq", axis=0, tiled=True).astype(
-            slot_den.dtype
-        ),
+        all_by_exchange(slot_den.astype(jnp.bfloat16), "seq", 0).astype(slot_den.dtype),
     )
     short_num = jnp.take(every_num, home_slot, axis=0)
     short_den = jnp.take(every_den, home_slot, axis=0)

time: 437 us -> 398 us (0.911)
  the two profiles are of different devices: /device:TPU:8 before, /device:TPU:4 now
where the time goes in v1:
time: 398 us
  blocking collectives  345 us (87%)
  between operations  14.3 us (4%)
  local copies, waits for them, and re-layouts  13.3 us (3%)
  matrix products  10.7 us (3%)
  other arithmetic  7.43 us (2%)
  starting transfers between devices  6.78 us (2%)
    psum x1, blocking collectives, on_device(): long_num, long_den = lax.psum((long_part_num, long_part_den), 'seq')  251 us
    all_gather x1, blocking collectives, on_device(): all_queries = lax.all_gather(query[:n_short], 'seq', axis=0, tiled=True)  52.6 us
    psum x1, blocking collectives, on_device(): proj = lax.psum(partial_proj.astype(jnp.bfloat16), 'tp').astype(jnp.float32)  17.1 us
    all_gather x1, blocking collectives, on_device(): lax.all_gather(short_hidden, 'tp', axis=1, tiled=True)  12.2 us
    all_gather x1, blocking collectives, on_device(): lax.all_gather(long_hidden, 'tp', axis=1, tiled=True)  12.1 us
  transfers between devices with their start and end apart: 2, of which 0 were waited for; matrix products, arithmetic and copies ran while one was open for 2% of the time, Pallas kernels for 0%

profile of v1, /device:TPU:4, one launch (start us, length us, event | category | flops | bytes accessed | tf_op | source)
XLA Modules:
  0.0 397.6 jit_solution(171430743132727998)
XLA Ops:
  7.3 1.0 fusion.5
  8.3 0.9 compare_reduce_fusion
  9.2 1.4 gather_fusion
  10.7 12.1 %all-gather.1 = bf16[4,320,4]{1,2,0:T(4,128)(2,1)S(1)} all-gather(bf16[1,320,4]{1,2,0:T(4,128)(2,1)} %bitcast.78), channel_id=1, replica_groups=mesh['seq'=64,'tp'=4] {'tp'}, dimensions={0}, use_global_device_ids=true | all-gather | bytes 12800 | tf_op jit(solution)/shard_map/all_gather | solution.py:66
  22.9 12.2 %all-gather = bf16[4,320,16]{1,2,0:T(8,128)(2,1)S(1)} all-gather(bf16[1,320,16]{1,2,0:T(8,128)(2,1)} %bitcast.77), channel_id=1, replica_groups=mesh['seq'=64,'tp'=4] {'tp'}, dimensions={0}, use_global_device_ids=true | all-gather | bytes 51200 | tf_op jit(solution)/shard_map/all_gather | solution.py:65
  35.2 1.5 fusion.39
  37.1 1.5 fusion.38
  38.9 52.6 %all_gather.14 = bf16[1024,320]{1,0:T(8,128)(2,1)S(1)} all-gather(bf16[16,320]{1,0:T(8,128)(2,1)S(1)} %slice.24), channel_id=1, replica_groups=mesh['seq'=64,'tp'=4] {'seq'}, dimensions={0}, use_global_device_ids=true | all-gather | bytes 665600 | tf_op jit(solution)/shard_map/all_gather | solution.py:79
  91.6 0.6 gather_fusion.1
  92.3 0.1 select_bitcast_fusion
  92.5 0.8 fusion.13
  93.3 0.1 fusion.17
  93.4 0.7 copy-done.3
  94.1 1.5 fusion.11
  95.5 0.7 convert_element_type.64
  96.3 0.7 stack.2
  96.9 6.7 %all-to-all-start = ((bf16[64,32,5]{1,2,0:T(8,128)(2,1)}), bf16[64,32,5]{1,2,0:T(8,128)(2,1)S(1)}, u32[]{:S(2)}, u32[]{:S(2)}) async-start(bf16[64,32,5]{1,2,0:T(8,128)(2,1)} %stack.2), calls=%async_computation | async-start | bytes 262144 | tf_op jit(solution)/shard_map/all_to_all | solution.py:14
  104.0 0.8 compare_and_fusion.1
  104.8 1.6 fusion.40
  106.5 1.8 fusion.19
  108.4 251.1 %all-reduce = (f32[4,5]{0,1:T(8,128)S(1)}, f32[4,320]{1,0:T(4,128)S(1)}) all-reduce(f32[4,5]{0,1:T(8,128)S(1)} %get-tuple-element.13, f32[4,320]{1,0:T(4,128)S(1)} %reshape.153), channel_id=1, replica_groups=mesh['seq'=64,'tp'=4] {'seq'}, use_global_device_ids=true, to_apply=%region_7.8 | all-reduce | flops 1300 | bytes 10400 | tf_op jit(solution)/shard_map/psum | solution.py:106
  359.6 0.1 copy.41
  359.7 1.8 copy.60
  361.5 1.8 gather_fusion.3
  364.1 3.3 convert_element_type.65
  367.4 2.5 gather_fusion.2
  369.9 2.1 convolution_convert_fusion
  372.1 17.1 %psum.23 = bf16[20,1280]{1,0:T(8,128)(2,1)S(1)} all-reduce(bf16[20,1280]{1,0:T(8,128)(2,1)S(1)} %convolution_convert_fusion), channel_id=1, replica_groups=mesh['seq'=64,'tp'=4] {'tp'}, use_global_device_ids=true, to_apply=%region_8.9 | all-reduce | flops 25600 | bytes 102400 | tf_op jit(solution)/shard_map/psum | solution.py:121
  389.1 0.1 fusion.7
  389.3 0.2 multiply_reduce_fusion
  389.6 0.6 slice.27
  390.2 0.6 slice.26
  (57 shorter events, 2.8 us)
Async XLA Ops:
  7.2 85.3 %copy-start = (bf16[32,128,320]{1,2,0:T(8,128)(2,1)S(1)}, bf16[32,128,320]{1,2,0:T(8,128)(2,1)}, u32[]{:S(2)}) copy-start(bf16[32,128,320]{1,2,0:T(8,128)(2,1)} %param.24) | copy-start | bytes 7864324
  7.2 31.7 %copy-start.2 = (f32[320]{0:T(512)S(1)}, f32[320]{0:T(512)}, u32[]{:S(2)}) copy-start(f32[320]{0:T(512)} %param.22) | copy-start | bytes 3844
  7.2 356.9 %all-gather.4.cloned.1.call-start = ((), (), s32[]{:S(2)}) async-start(), calls=%async_computation.1 | async-start | bytes 1597440 | tf_op jit(solution)/shard_map/all_gather | solution.py:96
  92.3 1.7 copy-start.3
  96.9 262.7 %all-to-all-start = ((bf16[64,32,5]{1,2,0:T(8,128)(2,1)}), bf16[64,32,5]{1,2,0:T(8,128)(2,1)S(1)}, u32[]{:S(2)}, u32[]{:S(2)}) async-start(bf16[64,32,5]{1,2,0:T(8,128)(2,1)} %stack.2), calls=%async_computation | async-start | bytes 262144 | tf_op jit(solution)/shard_map/all_to_all | solution.py:14
  364.1 25.2 %copy-start.1 = (f32[1280]{0:T(1024)S(1)}, f32[1280]{0:T(1024)}, u32[]{:S(2)}) copy-start(f32[1280]{0:T(1024)} %param.23) | copy-start | bytes 15364
Sparse Core Ops, SparseCore 0:
  96.4 75.4 all-gather.3
